TPU v7x, 128 devices: a whole 4x4x4 slice. The times are simulated.
128 devices in a mesh: leaf: 8 (over z, x_hi), ctx: 16 (over y, x_lo, core).
Axes of the slice: x: 4 (x_hi: 2, x_lo: 2; x = x_hi * 2 + x_lo), y: 4, z: 4, core: 2. Of those that a mesh axis runs over, the one named last changes fastest.
Arguments:
- queries: bfloat16 [16384, 8192], P(('leaf', 'ctx')), may hold values from -38 to 38, as said below
- seg_keys: bfloat16 [16384, 1024], P(('leaf', 'ctx')), may hold values from -6 to 6
- seg_values: bfloat16 [16384, 1024], P(('leaf', 'ctx')), may hold values from -6 to 6
- root_keys: bfloat16 [2048, 1024], P('ctx'), may hold values from -6 to 6, as said below
- root_values: bfloat16 [2048, 1024], P('ctx'), may hold values from -6 to 6
- expansion: int32 [2, 8], replicated, may hold values from 0 to 7, as said below
- root_offsets: int32 [8], replicated, may hold values from 512 to 2048
Outputs:
- attended: bfloat16 [16384, 8192], P(('leaf', 'ctx'))
Inputs may be any that keep to these rules, and one draw needn't show every extreme that they name: queries of order one, with some rows much larger. `root_keys`: keys of order one. `expansion`: group 8 - 1 is the root: it has depth 0 and is its own parent; every other group's parent has depth one less than its own.
All inputs are finite; a program needn't handle non-finite values.
Results may differ from a plain program's by a relative error of at most 0.0065.
Values may be sent and summed in bfloat16 or wider, within the bound.
A program may use at most 128 MiB of HBM per device.

v0:
```python
import math

import jax
import jax.numpy as jnp
from jax import lax
from jax.sharding import PartitionSpec as P

HQ = 64
KVH = 8
HD = 128


def on_device(queries, seg_keys, seg_values, root_keys, root_values, expansion, root_offsets):
    q_rows = queries.shape[0]
    group_width = HQ // KVH
    score_scale = 1.0 / math.sqrt(HD)
    group_idx = lax.axis_index("leaf")
    part_pos = lax.axis_index("ctx")
    parent = expansion[0, group_idx]
    tree_depth = expansion[1, group_idx]
    visible = root_offsets[group_idx]
    query_pos = part_pos * q_rows + jnp.arange(q_rows, dtype=jnp.int32)
    query_heads = queries.reshape(q_rows, KVH, group_width, HD).transpose(1, 2, 0, 3)

    def attend(state_now, key_rows, value_rows, allowed):
        run_max, run_sum, run_acc = state_now
        count_keys = key_rows.shape[0]
        key_grid = key_rows.reshape(count_keys, KVH, HD)
        value_grid = value_rows.reshape(count_keys, KVH, HD)

        def head_step(unused, item):
            head_index, head_query, old_max, old_sum, old_acc = item
            head_keys = lax.dynamic_index_in_dim(key_grid, head_index, 1, keepdims=False)
            head_values = lax.dynamic_index_in_dim(value_grid, head_index, 1, keepdims=False)
            scores = (
                jnp.einsum("gqd,kd->gqk", head_query, head_keys, preferred_element_type=jnp.float32)
                * score_scale
            )
            scores = jnp.where(allowed[None], scores, -1e30)
            new_max = jnp.maximum(old_max, jnp.max(scores, axis=-1))
            shrink = jnp.exp(old_max - new_max)
            weights = jnp.where(allowed[None], jnp.exp(scores - new_max[..., None]), 0.0)
            new_sum = old_sum * shrink + jnp.sum(weights, axis=-1)
            new_acc = old_acc * shrink[..., None] + jnp.einsum(
                "gqk,kd->gqd",
                weights.astype(jnp.bfloat16),
                head_values,
                preferred_element_type=jnp.float32,
            )
            return (unused, (new_max, new_sum, new_acc))

        head_ids = jnp.arange(KVH, dtype=jnp.int32)
        unused, updated = lax.scan(head_step, 0, (head_ids, query_heads, run_max, run_sum, run_acc))
        return updated

    every_key, every_value = (
        lax.all_gather(seg_keys, "leaf", axis=0, tiled=True),
        lax.all_gather(seg_values, "leaf", axis=0, tiled=True),
    )
    parent_keys = lax.dynamic_slice_in_dim(every_key, parent * q_rows, q_rows, 0)
    parent_values = lax.dynamic_slice_in_dim(every_value, parent * q_rows, q_rows, 0)
    initial = (
        jnp.full((KVH, group_width, q_rows), -1e30, jnp.float32),
        jnp.zeros((KVH, group_width, q_rows), jnp.float32),
        jnp.zeros((KVH, group_width, q_rows, HD), jnp.float32),
    )
    key_rows = lax.all_gather(root_keys, "ctx", axis=0, tiled=True)
    value_rows = lax.all_gather(root_values, "ctx", axis=0, tiled=True)
    count_keys = key_rows.shape[0]
    key_pos = jnp.arange(count_keys, dtype=jnp.int32)
    allowed = jnp.broadcast_to((key_pos < visible)[None, :], (q_rows, count_keys))
    state_now = attend(initial, key_rows, value_rows, allowed)
    key_rows = lax.all_gather(seg_keys, "ctx", axis=0, tiled=True)
    value_rows = lax.all_gather(seg_values, "ctx", axis=0, tiled=True)
    count_keys = key_rows.shape[0]
    key_pos = jnp.arange(count_keys, dtype=jnp.int32)
    allowed = key_pos[None, :] <= query_pos[:, None]
    state_now = attend(state_now, key_rows, value_rows, allowed)
    key_rows = lax.all_gather(parent_keys, "ctx", axis=0, tiled=True)
    value_rows = lax.all_gather(parent_values, "ctx", axis=0, tiled=True)
    count_keys = key_rows.shape[0]
    allowed = jnp.broadcast_to(tree_depth > 0, (q_rows, count_keys))
    state_now = attend(state_now, key_rows, value_rows, allowed)
    run_max, run_sum, run_acc = state_now
    blended = run_acc / run_sum[..., None]
    return blended.transpose(2, 0, 1, 3).reshape(q_rows, HQ * HD).astype(jnp.bfloat16)


def solution(mesh):
    return jax.shard_map(
        on_device,
        mesh=mesh,
        in_specs=(
            P(("leaf", "ctx"), None),
            P(("leaf", "ctx"), None),
            P(("leaf", "ctx"), None),
            P("ctx", None),
            P("ctx", None),
            P(),
            P(),
        ),
        out_specs=P(("leaf", "ctx"), None),
        check_vma=False,
    )
```

profile of v0, /device:TPU:1, one launch (start us, length us, event | category | flops | bytes accessed | tf_op | source)
XLA Modules:
  0.0 513.4 jit_solution(16176311262757333328)
XLA Ops:
  17.3 49.0 %all-gather.21.cloned.1.call-done = bf16[1024,1024]{0,1:T(8,128)(2,1)} async-done(((bf16[128,1024]{0,1:T(8,128)(2,1)}), bf16[1024,1024]{0,1:T(8,128)(2,1)}) %all-gather.21.cloned.1.call-update) | async-done | bytes 2097168 | tf_op jit(solution)/shard_map/all_gather | solution.py:58
  69.3 4.1 copy.9
  77.8 42.8 %all-gather.17.cloned.1.call-done = bf16[1024,1024]{0,1:T(8,128)(2,1)} async-done(((bf16[128,1024]{0,1:T(8,128)(2,1)}), bf16[1024,1024]{0,1:T(8,128)(2,1)}) %all-gather.17.cloned.1.call-update) | async-done | bytes 2097168 | tf_op jit(solution)/shard_map/all_gather | solution.py:57
  122.2 43.9 %all-gather.9.cloned.1.call-done = bf16[2048,1024]{0,1:T(8,128)(2,1)} async-done(((bf16[128,1024]{0,1:T(8,128)(2,1)}), bf16[2048,1024]{0,1:T(8,128)(2,1)}) %all-gather.9.cloned.1.call-update) | async-done | bytes 4194320 | tf_op jit(solution)/shard_map/all_gather | solution.py:67
  166.1 46.7 %all-gather.11.cloned.1.call-done = bf16[2048,1024]{0,1:T(8,128)(2,1)} async-done(((bf16[128,1024]{0,1:T(8,128)(2,1)}), bf16[2048,1024]{0,1:T(8,128)(2,1)}) %all-gather.11.cloned.1.call-update) | async-done | bytes 4194320 | tf_op jit(solution)/shard_map/all_gather | solution.py:68
  215.3 90.6 %while.43 = (s32[]{:T(128)}, f32[8,8,128]{2,1,0:T(8,128)S(1)}, f32[8,8,128]{2,1,0:T(8,128)S(1)}, f32[8,8,128,128]{3,2,1,0:T(8,128)}, bf16[8,8,128,128]{3,2,1,0:T...) while((s32[]{:T(128)}, f32[8,8,128]{2,1,0:T(8,128)S(1)}, ...), condition=%wide.region_3.4_spmd.clone, body=%wide.region_0.3_spmd.clone.sunk | while | flops 1101140992 | bytes 27057328 | solution.py:53
  220.3 4.1 fusion.124
  231.7 4.0 fusion.124
  243.1 4.0 fusion.124
  265.7 4.0 fusion.124
  277.0 4.1 fusion.124
  288.3 4.0 fusion.124
  299.7 4.0 fusion.124
  308.6 98.2 %while.44 = (s32[]{:T(128)}, f32[8,8,128]{2,1,0:T(8,128)S(1)}, f32[8,8,128]{2,1,0:T(8,128)S(1)}, f32[8,8,128,128]{3,2,1,0:T(8,128)}, f32[8,8,128]{2,1,0:T(8,128)...) while((s32[]{:T(128)}, f32[8,8,128]{2,1,0:T(8,128)S(1)}, ...), condition=%wide.region_7.8_spmd.clone, body=%wide.region_4.7_spmd.clone.sunk | while | flops 1101533184 | bytes 28636876 | solution.py:53
  314.0 4.3 fusion.131
  326.2 4.4 fusion.131
  338.6 4.4 fusion.131
  350.8 4.3 fusion.131
  363.1 4.4 fusion.131
  375.4 4.3 fusion.131
  387.6 4.3 fusion.131
  399.9 4.3 fusion.131
  409.3 89.9 %while.45 = (s32[]{:T(128)}, f32[8,8,128]{2,1,0:T(8,128)S(1)}, f32[8,8,128,128]{3,2,1,0:T(8,128)}, f32[8,8,128]{2,1,0:T(8,128)S(1)}, f32[8,8,128]{2,1,0:T(8,128)...) while((s32[]{:T(128)}, f32[8,8,128]{2,1,0:T(8,128)S(1)}, ...), condition=%wide.region_11.12_spmd.clone, body=%wide.region_8.11_spmd.clone.sunk | while | flops 1101271040 | bytes 27584708 | solution.py:53
  470.5 4.0 fusion.138
  (181 shorter events, 198.5 us)
Async XLA Ops:
  6.5 59.8 %all-gather.21.cloned.1.call-start = ((), (), s32[]{:S(2)}) async-start(), calls=%async_computation.6 | async-start | bytes 2359296 | tf_op jit(solution)/shard_map/all_gather | solution.py:58
  8.4 112.2 %all-gather.17.cloned.1.call-start = ((), (), s32[]{:S(2)}) async-start(), calls=%async_computation.4 | async-start | bytes 2359296 | tf_op jit(solution)/shard_map/all_gather | solution.py:57
  10.2 155.9 %all-gather.9.cloned.1.call-start = ((), (), s32[]{:S(2)}) async-start(), calls=%async_computation | async-start | bytes 4456448 | tf_op jit(solution)/shard_map/all_gather | solution.py:67
  12.1 200.7 %all-gather.11.cloned.1.call-start = ((), (), s32[]{:S(2)}) async-start(), calls=%async_computation.1 | async-start | bytes 4456448 | tf_op jit(solution)/shard_map/all_gather | solution.py:68
  14.0 291.9 %all-gather.13.cloned.1.call-start = ((), (), s32[]{:S(2)}) async-start(), calls=%async_computation.2 | async-start | bytes 4456448 | tf_op jit(solution)/shard_map/all_gather | solution.py:73
  14.6 291.5 %all-gather.15.cloned.1.call-start = ((), (), s32[]{:S(2)}) async-start(), calls=%async_computation.3 | async-start | bytes 4456448 | tf_op jit(solution)/shard_map/all_gather | solution.py:74
  15.2 391.6 %all-gather.23.cloned.1.call-start = ((), (), s32[]{:S(2)}) async-start(), calls=%async_computation.7 | async-start | bytes 4456448 | tf_op jit(solution)/shard_map/all_gather | solution.py:80
  68.0 338.8 %all-gather.19.cloned.1.call-start = ((), (), s32[]{:S(2)}) async-start(), calls=%async_computation.5 | async-start | bytes 4456448 | tf_op jit(solution)/shard_map/all_gather | solution.py:79
Sparse Core Ops, SparseCore 0:
  9.5 56.7 all-gather.20
  68.5 52.0 all-gather.16
  122.2 43.8 all-gather.8
  167.6 45.1 all-gather.10
  214.2 45.1 all-gather.12
  260.9 45.1 all-gather.14
  307.7 45.1 all-gather.22
  354.5 45.0 all-gather.18
where the time goes:
time: 516 us; the launch traced here: 513 us
  waiting for transfers between devices  184 us (36%)
  matrix products  161 us (31%)
  other arithmetic  60.6 us (12%)
  local copies, waits for them, and re-layouts  46.9 us (9%)
  loops' own time  46.4 us (9%)
  between operations  15 us (3%)
    dot_general x24, matrix products, head_step(): jnp.einsum('gqk,kd->gqd', weights.astype(jnp.bfloat16), head_values, pref...  99.1 us
    dot_general x24, matrix products, head_step(): jnp.einsum('gqd,kd->gqk', head_query, head_keys, preferred_element_type=j...  61.4 us
    reduce_sum x24, other arithmetic, head_step(): new_sum = old_sum * shrink + jnp.sum(weights, axis=-1)  54.8 us
    all_gather x1, waiting for transfers between devices, on_device(): lax.all_gather(seg_values, 'leaf', axis=0, tiled=True)  49 us
    all_gather x1, waiting for transfers between devices, on_device(): value_rows = lax.all_gather(root_values, 'ctx', axis=0, tiled=True)  46.7 us
    another operation x3, loops' own time, attend(): lax.scan(head_step, 0, (head_ids, query_heads, run_max, run_sum, run_acc))  46.4 us
    all_gather x1, waiting for transfers between devices, on_device(): key_rows = lax.all_gather(root_keys, 'ctx', axis=0, tiled=True)  43.9 us
    all_gather x1, waiting for transfers between devices, on_device(): lax.all_gather(seg_keys, 'leaf', axis=0, tiled=True)  42.8 us
  transfers between devices with their start and end apart: 8, of which 5 were waited for; matrix products, arithmetic and copies ran while one was open for 36% of the time, Pallas kernels for 0%

commit v1 on v0

v1 whole, which is shorter than its diff:
```python
import functools
import math

import jax
import jax.numpy as jnp
from jax import lax
from jax.experimental import pallas as pl
from jax.experimental.pallas import tpu as pltpu
from jax.sharding import PartitionSpec as P

HQ = 64
KVH = 8
HD = 128
MESH = pl.DeviceIdType.MESH
SCALE = math.log2(math.e) / math.sqrt(HD)
LOW = -1e30

ROOT, OWN, PAR = 0, 1, 2
ORDERS = ((0, 1, 2), (1, 2, 0), (2, 0, 1))


def order_of(source, part):
    return ORDERS[part] if part < 3 else ORDERS[source]


N_PARTNER = 9
N_STEP = 36
N_LEAF = 5
N_OUT = 4
BASE_STEP = N_PARTNER
BASE_LEAF = BASE_STEP + N_STEP
BASE_OUT = BASE_LEAF + N_LEAF
N_COPIES = BASE_OUT + N_OUT
N_LOCAL = 14
KB = 1024
RB = 512


def kernel(expansion, offsets, q_hbm, k_hbm, v_hbm, rk_hbm, rv_hbm, o_hbm,
           kv, qbuf, zbuf, pick, got, acc, top, den, bound, stage, send_sem, recv_sem, local_sem):
    leaf, ctx = lax.axis_index("leaf"), lax.axis_index("ctx")
    z, xh = leaf // 2, leaf % 2
    y, c, k = ctx // 4, (ctx // 2) % 2, ctx % 2
    a, b = ((y + 1) // 2) % 2, y // 2
    d, e = ((z + 1) // 2) % 2, z // 2
    partner = (leaf, ctx + 1 - 2 * k)
    near = (
        (leaf, ctx + 4 - 8 * (y % 2)),
        (leaf, (3 - y) * 4 + c * 2 + k),
        (leaf, ctx + 2 - 4 * c),
    )
    near_d = ((z + 1 - 2 * (z % 2)) * 2 + xh, ctx)
    near_e = ((3 - z) * 2 + xh, ctx)
    near_f = (leaf + 1 - 2 * xh, ctx + 2 - 4 * c)

    barrier = pltpu.get_barrier_semaphore()
    for other in (partner, *near, near_d, near_e, near_f):
        pl.semaphore_signal(barrier, inc=1, device_id=other, device_id_type=MESH)
    pl.semaphore_wait(barrier, 7)

    def remote(src, dst, number, device):
        return pltpu.make_async_remote_copy(
            src_ref=src, dst_ref=dst, send_sem=send_sem.at[number], recv_sem=recv_sem.at[number],
            device_id=device, device_id_type=MESH,
        )

    mine512 = pl.ds(pl.multiple_of(k * 512, 128), 512)
    other512 = pl.ds(pl.multiple_of((1 - k) * 512, 128), 512)
    mine4096 = pl.ds(pl.multiple_of(k * 4096, 128), 4096)
    other4096 = pl.ds(pl.multiple_of((1 - k) * 4096, 128), 4096)
    mine128 = pl.ds(pl.multiple_of(k * 128, 128), 128)
    other128 = pl.ds(pl.multiple_of((1 - k) * 128, 128), 128)

    def pair_copies(source, number, arrays):
        sends, locals_ = [], []
        for t, array in enumerate(arrays):
            for j in range(2):
                rows = pl.ds(64 * j, 64)
                slot = kv.at[source, 2 * k + j, a, b, c, t]
                n = number + 2 * t + j
                sends.append(remote(array.at[rows, other512], slot, n, partner))
                locals_.append(pltpu.make_async_copy(array.at[rows, mine512], slot, local_sem.at[n]))
        return sends, locals_

    root_sends, root_locals = pair_copies(ROOT, 0, (rk_hbm, rv_hbm))
    own_sends, own_locals = pair_copies(OWN, 4, (k_hbm, v_hbm))
    q_send = remote(q_hbm.at[:, other4096], qbuf.at[mine128, :], 8, partner)
    q_local = pltpu.make_async_copy(q_hbm.at[:, mine4096], qbuf.at[mine128, :], local_sem.at[8])
    for copy in (*root_sends, *root_locals, *own_sends, *own_locals, q_send, q_local):
        copy.start()

    bits = (a, b, c)

    def step_copies(source, step):
        copies = []
        for part in range(4):
            order = order_of(source, part)
            have = order[:step]
            where = [slice(None) if dim in have else bits[dim] for dim in range(3)]
            slot = kv.at[source, part, where[0], where[1], where[2]]
            n = BASE_STEP + source * 12 + step * 4 + part
            copies.append(remote(slot, slot, n, near[order[step]]))
        return copies

    steps = {(s, t): step_copies(s, t) for s in range(3) for t in range(3)}

    def start(copies):
        for copy in copies:
            copy.start()

    def arrive(copies):
        for copy in copies:
            copy.wait_recv()

    def wait_all(copies):
        for copy in copies:
            copy.wait()

    leaf1 = [
        remote(kv.at[OWN, 0:2, a, b, c], zbuf.at[d, e, 0:2], BASE_LEAF, near_d),
        remote(kv.at[OWN, 2:4, a, b, c], zbuf.at[d, e, 2:4], BASE_LEAF + 1, near_e),
    ]
    leaf_local = pltpu.make_async_copy(kv.at[OWN, :, a, b, c], zbuf.at[d, e], local_sem.at[9])
    leaf2 = [
        remote(zbuf.at[:, e, 0:2], zbuf.at[:, e, 0:2], BASE_LEAF + 2, near_e),
        remote(zbuf.at[d, :, 2:4], zbuf.at[d, :, 2:4], BASE_LEAF + 3, near_d),
    ]
    leaf3 = [remote(pick, got, BASE_LEAF + 4, near_f)]

    arrive(root_sends)
    wait_all(root_locals)
    start(steps[ROOT, 0])
    arrive(own_sends)
    wait_all(own_locals)
    start(leaf1)
    start(steps[OWN, 0])
    leaf_local.start()

    acc[...] = jnp.zeros(acc.shape, jnp.float32)
    den[...] = jnp.zeros(den.shape, jnp.float32)
    top[...] = jnp.full(top.shape, LOW, jnp.float32)

    arrive(steps[ROOT, 0])
    start(steps[ROOT, 1])
    arrive(steps[OWN, 0])
    start(steps[OWN, 1])
    leaf_local.wait()
    arrive(leaf1)
    start(leaf2)
    arrive([q_send])
    q_local.wait()
    arrive(steps[ROOT, 1])
    start(steps[ROOT, 2])

    parent, depth, visible = expansion[0, leaf], expansion[1, leaf], offsets[leaf]
    parent_f = expansion[0, near_f[0]]
    row_pos = y * 512 + c * 256

    def unit_of(group, part, t):
        zg = group // 2
        return zbuf[((zg + 1) // 2) % 2, zg // 2, part, t]

    def choose_for_f():
        for part in range(4):
            for t in range(2):
                pick[part, t] = unit_of(parent_f, part, t)

    def choose_parent():
        here = (parent % 2) == xh
        for part in range(4):
            for t in range(2):
                kv[PAR, part, a, b, c, t] = jnp.where(here, unit_of(parent, part, t), got[part, t])

    out_cols = [pl.ds(pl.multiple_of((k * 4 + h) * 1024, 128), 1024) for h in range(4)]
    back_cols = [pl.ds(pl.multiple_of(((1 - k) * 4 + h) * 1024, 128), 1024) for h in range(4)]
    out_sends = [
        remote(stage.at[other128, h * 1024:(h + 1) * 1024], o_hbm.at[:, out_cols[h]], BASE_OUT + h, partner)
        for h in range(4)
    ]
    out_locals = [
        pltpu.make_async_copy(stage.at[mine128, h * 1024:(h + 1) * 1024], o_hbm.at[:, out_cols[h]], local_sem.at[10 + h])
        for h in range(4)
    ]

    def send_head(h):
        out_sends[h].start()
        out_locals[h].start()

    hooks = {
        1: lambda: (arrive(steps[OWN, 1]), start(steps[OWN, 2])),
        2: lambda: (arrive(leaf2), choose_for_f()),
        3: lambda: start(leaf3),
        4: lambda: arrive(steps[ROOT, 2]),
        7: lambda: (arrive(leaf3), choose_parent()),
        8: lambda: (start(steps[PAR, 0]), arrive(steps[OWN, 2])),
        10: lambda: (arrive(steps[PAR, 0]), start(steps[PAR, 1])),
        13: lambda: (arrive(steps[PAR, 1]), start(steps[PAR, 2])),
        20: lambda: arrive(steps[PAR, 2]),
        21: lambda: send_head(0),
        22: lambda: send_head(1),
        23: lambda: send_head(2),
    }

    lane = lax.broadcasted_iota(jnp.int32, (1, 128), 1)

    def one(it, carry):
        for number, act in hooks.items():
            @pl.when(it == number)
            def _():
                act()
        chunk, h = it // 4, it % 4
        source, half = chunk // 2, chunk % 2
        is_own = source == OWN
        columns = pl.ds(pl.multiple_of(h * HD, HD), HD)

        pieces = []
        for part in range(4):
            lasts = [order_of(s, part)[2] for s in range(3)]
            fixed = jnp.where(is_own, 1, jnp.where(source == ROOT, lasts[ROOT], lasts[PAR]))
            own_bit = jnp.where(fixed == 0, a, jnp.where(fixed == 1, b, c))
            bit = jnp.where(is_own, half, (own_bit + half) % 2)
            for j in range(4):
                j1, j0 = j // 2, j % 2
                pa = jnp.where(fixed == 0, bit, j1)
                pb = jnp.where(fixed == 1, bit, jnp.where(fixed == 0, j1, j0))
                pc = jnp.where(fixed == 2, bit, j0)
                plane = 2 * pb + pa + pb - 2 * pa * pb
                pieces.append((part, pa, pb, pc, plane * 512 + pc * 256 + part * 64))

        @pl.when(h == 0)
        def _():
            limit = jnp.where(source == ROOT, visible, jnp.where(depth > 0, 4096, 0))
            rows = lax.broadcasted_iota(jnp.int32, (256, 1), 0) + row_pos + 1
            limits = jnp.where(is_own, rows, limit)
            for j in range(8):
                base = jnp.where(lane < 64, pieces[2 * j][4] + lane, pieces[2 * j + 1][4] + lane - 64)
                bound[:, j * 128:(j + 1) * 128] = jnp.where(base < limits, 1e38, LOW)

        keys = jnp.concatenate([kv[source, p, pa, pb, pc, 0, :, columns] for p, pa, pb, pc, _ in pieces], 0)
        values = jnp.concatenate([kv[source, p, pa, pb, pc, 1, :, columns] for p, pa, pb, pc, _ in pieces], 0)
        values = jnp.concatenate([values, jnp.ones((KB, HD), jnp.bfloat16)], 1)

        def score(sb):
            rows = [
                qbuf[:, pl.ds(pl.multiple_of((h * 8 + 2 * sb + i) * HD, HD), HD)] for i in range(2)
            ]
            return lax.dot_general(
                jnp.concatenate(rows, 0), keys, (((1,), (1,)), ((), ())), preferred_element_type=jnp.float32
            )

        def soften(sb, s):
            rows = pl.ds(sb * RB, RB)
            old = top[h, rows, :]
            limited, best = [], None
            for j in range(KB // 128):
                lim = bound[:, j * 128:(j + 1) * 128]
                sj = jnp.minimum(s[:, j * 128:(j + 1) * 128], jnp.concatenate([lim, lim], 0))
                limited.append(sj)
                best = sj if best is None else jnp.maximum(best, sj)
            new = jnp.maximum(old, jnp.max(best, axis=1, keepdims=True))
            shrink = jnp.exp2((old - new) * SCALE)
            shift = new * SCALE
            weights = jnp.concatenate([jnp.exp2(sj * SCALE - shift).astype(jnp.bfloat16) for sj in limited], 1)
            out = jnp.dot(weights, values, preferred_element_type=jnp.float32)
            den[h, rows, :] = den[h, rows, :] * shrink + out[:, HD:]
            acc[h, rows, :] = acc[h, rows, :] * shrink + out[:, :HD]
            top[h, rows, :] = new

        s = score(0)
        for sb in range(4):
            following = score(sb + 1) if sb < 3 else None
            soften(sb, s)
            s = following

        @pl.when(chunk == 5)
        def _():
            for g in range(8):
                rows = pl.ds(g * 256, 256)
                cols = pl.ds(pl.multiple_of((h * 8 + g) * HD, HD), HD)
                stage[:, cols] = (acc[h, rows, :] / den[h, rows, :]).astype(jnp.bfloat16)

        return carry

    lax.fori_loop(0, 24, one, 0)
    send_head(3)

    for copies in (root_sends, own_sends, [q_send], leaf1, leaf2, leaf3, *steps.values()):
        for copy in copies:
            copy.wait_send()
    wait_all(out_sends)
    wait_all(out_locals)


def on_device(queries, seg_keys, seg_values, root_keys, root_values, expansion, root_offsets):
    smem = pl.BlockSpec(memory_space=pltpu.SMEM)
    anywhere = pl.BlockSpec(memory_space=pl.ANY)
    return pl.pallas_call(
        kernel,
        out_shape=jax.ShapeDtypeStruct(queries.shape, jnp.bfloat16),
        in_specs=[smem, smem] + [anywhere] * 5,
        out_specs=anywhere,
        scratch_shapes=[
            pltpu.VMEM((3, 4, 2, 2, 2, 2, 64, 512), jnp.bfloat16),
            pltpu.VMEM((256, 4096), jnp.bfloat16),
            pltpu.VMEM((2, 2, 4, 2, 64, 512), jnp.bfloat16),
            pltpu.VMEM((4, 2, 64, 512), jnp.bfloat16),
            pltpu.VMEM((4, 2, 64, 512), jnp.bfloat16),
            pltpu.VMEM((4, 2048, HD), jnp.float32),
            pltpu.VMEM((4, 2048, HD), jnp.float32),
            pltpu.VMEM((4, 2048, HD), jnp.float32),
            pltpu.VMEM((256, KB), jnp.float32),
            pltpu.VMEM((256, 4096), jnp.bfloat16),
            pltpu.SemaphoreType.DMA((N_COPIES,)),
            pltpu.SemaphoreType.DMA((N_COPIES,)),
            pltpu.SemaphoreType.DMA((N_LOCAL,)),
        ],
        compiler_params=pltpu.CompilerParams(
            collective_id=0, has_side_effects=True, vmem_limit_bytes=60 * 1024 * 1024
        ),
    )(expansion, root_offsets, queries, seg_keys, seg_values, root_keys, root_values)


def solution(mesh):
    return jax.shard_map(
        on_device,
        mesh=mesh,
        in_specs=(
            P(("leaf", "ctx"), None),
            P(("leaf", "ctx"), None),
            P(("leaf", "ctx"), None),
            P("ctx", None),
            P("ctx", None),
            P(),
            P(),
        ),
        out_specs=P(("leaf", "ctx"), None),
        check_vma=False,
    )
```

time: 516 us -> 134 us (0.26)
  waiting for transfers between devices: 184 us -> 0 us
  matrix products: 161 us -> 0 us
  Pallas kernels: 0 us -> 131 us
  other arithmetic: 60.6 us -> 0 us
  loops' own time: 46.4 us -> 0 us
  local copies, waits for them, and re-layouts: 46.9 us -> 3.1 us
  between operations: 15 us -> 0.01 us
    all_gather x8 -> x0, waiting for transfers between devices: 183 us -> none  [the longest x1 49 us: on_device(): lax.all_gather(seg_values, 'leaf', axis=0, tiled=True)]
    dot_general x48 -> x0, matrix products: 161 us -> none  [the longest x24 99.1 us: head_step(): jnp.einsum('gqk,kd->gqd', weights.astype(jnp.bfloat16), head_values, pref...]
    pallas_call x0 -> x1, Pallas kernels: none -> 131 us  [on_device(): pl.pallas_call(kernel, out_shape=jax.ShapeDtypeStruct(queries.shape, jnp....]
    reduce_sum x24 -> x0, other arithmetic: 54.8 us -> none  [head_step(): new_sum = old_sum * shrink + jnp.sum(weights, axis=-1)]
    another operation x3 -> x0, loops' own time: 46.4 us -> none  [attend(): lax.scan(head_step, 0, (head_ids, query_heads, run_max, run_sum, run_acc))]
    dynamic_slice x28 -> x0, local copies, waits for them, and re-layouts: 20.7 us -> none  [the longest x24 14.6 us: attend(): lax.scan(head_step, 0, (head_ids, query_heads, run_max, run_sum, run_acc))]
    unnamed x7 -> x1, local copies, waits for them, and re-layouts: 17.4 us -> 3.1 us
    another operation x8 -> x0, local copies, waits for them, and re-layouts: 7.44 us -> none
  transfers between devices with their start and end apart: 8 -> 0, of which waited for: 5 -> 0; matrix products, arithmetic and copies ran while one was open for 36% -> 0% of each run, Pallas kernels for 0% -> 0%
where the time goes in v1:
time: 134 us
  Pallas kernels  131 us (98%)
  local copies, waits for them, and re-layouts  3.1 us (2%)
    pallas_call x1, Pallas kernels, on_device(): pl.pallas_call(kernel, out_shape=jax.ShapeDtypeStruct(queries.shape, jnp....  131 us
    unnamed x1, local copies, waits for them, and re-layouts  3.1 us

profile of v1, /device:TPU:1, one launch (start us, length us, event | category | flops | bytes accessed | tf_op | source)
XLA Modules:
  0.0 133.8 jit_solution(2597466552463229305)
XLA Ops:
  0.0 130.7 %shard_map.73 = bf16[128,8192]{1,0:T(8,128)(2,1)} custom-call(s32[2,8]{1,0:T(2,128)} %expansion.1, s32[8]{0:T(128)} %offsets.1, bf16[128,8192]{1,0:T(8,128)(2,1)} %q_hbm.1, bf16[128,1024]{1,0:T(8,128)(2,1)} %k_hbm.1, bf16[128,1024]{1,0:T(8,128)(2,1)} %v_hbm.1, bf16[128,1024]{1,0:T(8,128)(2,1)} %rk_hbm.1, bf16[128,1024]{1,0:T(8,128)(2,1)} %rv_hbm.1), custom_call_target="tpu_custom_call" | custom-call | tf_op jit(solution)/shard_map/pallas_call | solution.py:297
  130.7 3.1 %copy.9 = bf16[128,8192]{1,0:T(8,128)(2,1)} copy(bf16[128,8192]{1,0:T(8,128)(2,1)} %shard_map.73) | data formatting | bytes 4194304

commit v2 on v1

v2 whole, which is shorter than its diff:
```python
import functools
import math

import jax
import jax.numpy as jnp
from jax import lax
from jax.experimental import pallas as pl
from jax.experimental.pallas import tpu as pltpu
from jax.sharding import PartitionSpec as P

HQ = 64
KVH = 8
HD = 128
MESH = pl.DeviceIdType.MESH
SCALE = math.log2(math.e) / math.sqrt(HD)
LOW = -1e30

ROOT, OWN, PAR = 0, 1, 2
PARTS = ((0, 80), (80, 96), (176, 80))
ORDERS = ((0, 1, 2), (1, 2, 0), (2, 0, 1))


def order_of(source, part):
    return ORDERS[(part + source) % 3]


N_COPIES = 61
N_LOCAL = 14
KB = 1024
RB = 512


def kernel(expansion, offsets, q_hbm, k_hbm, v_hbm, rk_hbm, rv_hbm, o_hbm,
           kv, qbuf, zbuf, pick, got, acc, top, den, bound, stage, send_sem, recv_sem, local_sem):
    leaf, ctx = lax.axis_index("leaf"), lax.axis_index("ctx")
    z, xh = leaf // 2, leaf % 2
    y, c, k = ctx // 4, (ctx // 2) % 2, ctx % 2
    a, b = ((y + 1) // 2) % 2, y // 2
    d, e = ((z + 1) // 2) % 2, z // 2
    partner = (leaf, ctx + 1 - 2 * k)
    near = (
        (leaf, ctx + 4 - 8 * (y % 2)),
        (leaf, (3 - y) * 4 + c * 2 + k),
        (leaf, ctx + 2 - 4 * c),
    )
    near_d = ((z + 1 - 2 * (z % 2)) * 2 + xh, ctx)
    near_e = ((3 - z) * 2 + xh, ctx)
    near_f = (leaf + 1 - 2 * xh, ctx + 2 - 4 * c)

    barrier = pltpu.get_barrier_semaphore()
    for other in (partner, *near, near_d, near_e, near_f):
        pl.semaphore_signal(barrier, inc=1, device_id=other, device_id_type=MESH)
    pl.semaphore_wait(barrier, 7)

    numbers = iter(range(N_COPIES))

    def remote(src, dst, device):
        number = next(numbers)
        return pltpu.make_async_remote_copy(
            src_ref=src, dst_ref=dst, send_sem=send_sem.at[number], recv_sem=recv_sem.at[number],
            device_id=device, device_id_type=MESH,
        )

    mine512 = pl.ds(pl.multiple_of(k * 512, 128), 512)
    other512 = pl.ds(pl.multiple_of((1 - k) * 512, 128), 512)
    mine4096 = pl.ds(pl.multiple_of(k * 4096, 128), 4096)
    other4096 = pl.ds(pl.multiple_of((1 - k) * 4096, 128), 4096)
    mine128 = pl.ds(pl.multiple_of(k * 128, 128), 128)
    other128 = pl.ds(pl.multiple_of((1 - k) * 128, 128), 128)

    def pair_copies(source, number, arrays):
        sends, locals_ = [], []
        for t, array in enumerate(arrays):
            slot = kv.at[source, a, b, c, t, mine128, :]
            sends.append(remote(array.at[:, other512], slot, partner))
            locals_.append(pltpu.make_async_copy(array.at[:, mine512], slot, local_sem.at[number + t]))
        return sends, locals_

    root_sends, root_locals = pair_copies(ROOT, 0, (rk_hbm, rv_hbm))
    own_sends, own_locals = pair_copies(OWN, 2, (k_hbm, v_hbm))
    q_send = remote(q_hbm.at[:, other4096], qbuf.at[mine128, :], partner)
    q_local = pltpu.make_async_copy(q_hbm.at[:, mine4096], qbuf.at[mine128, :], local_sem.at[8])
    for copy in (*root_sends, *root_locals, *own_sends, *own_locals, q_send, q_local):
        copy.start()

    bits = (a, b, c)

    def block(source, part, where, t=slice(None)):
        first, count = PARTS[part]
        return kv.at[source, where[0], where[1], where[2], t, first:first + count, :]

    both = slice(None)

    def double(source, part, step, second=None):
        order = order_of(source, part)
        where = {dim: both if dim in order[:step] else bits[dim] for dim in range(3)}
        if second is not None:
            where[order[1]] = second
        slot = block(source, part, where)
        return remote(slot, slot, near[order[step]])

    steps = {}
    for source in (ROOT, OWN, PAR):
        for step in (0, 1):
            steps[source, step] = [double(source, part, step) for part in range(3)]
    for source in (OWN, PAR):
        steps[source, 2] = [double(source, p, 2, bits[order_of(source, p)[1]]) for p in range(3)]
        steps[source, 3] = [double(source, p, 2, 1 - bits[order_of(source, p)[1]]) for p in range(3)]

    def shared(part, first, second, last, t=both):
        order = order_of(ROOT, part)
        where = {order[0]: first, order[1]: second, order[2]: last}
        return block(ROOT, part, where, t)

    quarter, round1, round2 = [], [], []
    for part in range(3):
        last = order_of(ROOT, part)[2]
        slot = shared(part, d, e, bits[last])
        quarter.append(remote(slot, slot, near[last]))
        flip = 1 - bits[last]
        for t, (one_way, other_way) in enumerate(((near_d, near_e), (near_e, near_d))):
            slot = shared(part, d, e, flip, t)
            round1.append(remote(slot, slot, one_way))
            slot = shared(part, both, e, flip, t) if t == 0 else shared(part, d, both, flip, t)
            round2.append(remote(slot, slot, other_way))

    def start(copies):
        for copy in copies:
            copy.start()

    def arrive(copies):
        for copy in copies:
            copy.wait_recv()

    def relay(arriving, leaving):
        for before, after in zip(arriving, leaving):
            before.wait_recv()
            after.start()

    def wait_all(copies):
        for copy in copies:
            copy.wait()

    low, high = slice(0, 128), slice(128, 256)
    leaf1 = [
        remote(kv.at[OWN, a, b, c, :, low, :], zbuf.at[d, e, :, low, :], near_d),
        remote(kv.at[OWN, a, b, c, :, high, :], zbuf.at[d, e, :, high, :], near_e),
    ]
    leaf_local = pltpu.make_async_copy(kv.at[OWN, a, b, c], zbuf.at[d, e], local_sem.at[9])
    leaf2 = [
        remote(zbuf.at[:, e, :, low, :], zbuf.at[:, e, :, low, :], near_e),
        remote(zbuf.at[d, :, :, high, :], zbuf.at[d, :, :, high, :], near_d),
    ]
    leaf3 = [remote(pick, got, near_f)]

    arrive(root_sends)
    wait_all(root_locals)
    start(steps[ROOT, 0])
    arrive(own_sends)
    wait_all(own_locals)
    start(leaf1)
    start(steps[OWN, 0])
    leaf_local.start()

    acc[...] = jnp.zeros(acc.shape, jnp.float32)
    den[...] = jnp.zeros(den.shape, jnp.float32)
    top[...] = jnp.full(top.shape, LOW, jnp.float32)

    leaf_local.wait()
    arrive([q_send])
    q_local.wait()

    parent, depth, visible = expansion[0, leaf], expansion[1, leaf], offsets[leaf]
    parent_f = expansion[0, near_f[0]]
    row_pos = y * 512 + c * 256

    def unit_of(group, t):
        zg = group // 2
        return zbuf[((zg + 1) // 2) % 2, zg // 2, t]

    def choose_for_f():
        for t in range(2):
            pick[t] = unit_of(parent_f, t)

    def choose_parent():
        here = (parent % 2) == xh
        for t in range(2):
            kv[PAR, a, b, c, t] = jnp.where(here, unit_of(parent, t), got[t])

    out_cols = [pl.ds(pl.multiple_of((k * 4 + h) * 1024, 128), 1024) for h in range(4)]
    back_cols = [pl.ds(pl.multiple_of(((1 - k) * 4 + h) * 1024, 128), 1024) for h in range(4)]
    out_sends = [
        remote(stage.at[other128, h * 1024:(h + 1) * 1024], o_hbm.at[:, out_cols[h]], partner)
        for h in range(4)
    ]
    out_locals = [
        pltpu.make_async_copy(stage.at[mine128, h * 1024:(h + 1) * 1024], o_hbm.at[:, out_cols[h]], local_sem.at[10 + h])
        for h in range(4)
    ]

    def send_head(h):
        out_sends[h].start()
        out_locals[h].start()

    def do(hooks, it):
        for number, act in hooks.items():
            @pl.when(it == number)
            def _():
                act()

    def piece(part, values):
        first, count = PARTS[part]
        pa, pb, pc = (values[dim] for dim in range(3))
        plane = 2 * pb + pa + pb - 2 * pa * pb
        return first, count, pa, pb, pc, plane * 512 + pc * 256 + first

    def attend(pieces, source, h, kb):
        columns = pl.ds(pl.multiple_of(h * HD, HD), HD)

        @pl.when(h == 0)
        def _():
            if source == ROOT:
                limits = visible
            elif source == OWN:
                limits = lax.broadcasted_iota(jnp.int32, (256, 1), 0) + row_pos + 1
            else:
                limits = jnp.where(depth > 0, 4096, 0)
            column = lax.broadcasted_iota(jnp.int32, (1, kb), 1)
            base, at = None, 0
            for first, count, _, _, _, position in pieces:
                here = position - at + column
                base = here if base is None else jnp.where(column >= at, here, base)
                at += count
            bound[:, :kb] = jnp.broadcast_to(jnp.where(base < limits, 1e38, LOW), (256, kb))

        def gather(t):
            return jnp.concatenate(
                [kv[source, pa, pb, pc, t, first:first + count, columns] for first, count, pa, pb, pc, _ in pieces], 0
            )

        keys = gather(0)
        values = jnp.concatenate([gather(1), jnp.ones((kb, HD), jnp.bfloat16)], 1)

        def score(sb):
            rows = [
                qbuf[:, pl.ds(pl.multiple_of((h * 8 + 2 * sb + i) * HD, HD), HD)] for i in range(2)
            ]
            return lax.dot_general(
                jnp.concatenate(rows, 0), keys, (((1,), (1,)), ((), ())), preferred_element_type=jnp.float32
            )

        def soften(sb, s):
            rows = pl.ds(sb * RB, RB)
            old = top[h, rows, :]
            limited, best = [], None
            for j in range(kb // 128):
                lim = bound[:, j * 128:(j + 1) * 128]
                sj = jnp.minimum(s[:, j * 128:(j + 1) * 128], jnp.concatenate([lim, lim], 0))
                limited.append(sj)
                best = sj if best is None else jnp.maximum(best, sj)
            new = jnp.maximum(old, jnp.max(best, axis=1, keepdims=True))
            shrink = jnp.exp2((old - new) * SCALE)
            shift = new * SCALE
            weights = jnp.concatenate([jnp.exp2(sj * SCALE - shift).astype(jnp.bfloat16) for sj in limited], 1)
            out = jnp.dot(weights, values, preferred_element_type=jnp.float32)
            den[h, rows, :] = den[h, rows, :] * shrink + out[:, HD:]
            acc[h, rows, :] = acc[h, rows, :] * shrink + out[:, :HD]
            top[h, rows, :] = new

        s = score(0)
        for sb in range(4):
            following = score(sb + 1) if sb < 3 else None
            soften(sb, s)
            s = following

    def pieces_of(source, firsts, seconds, last):
        pieces = []
        for part in range(3):
            order = order_of(source, part)
            for first in firsts:
                for second in seconds:
                    own = {dim: bits[dim] for dim in range(3)}
                    values = {
                        order[0]: first,
                        order[1]: second if isinstance(second, int) else (own[order[1]] + second[0]) % 2,
                        order[2]: (own[order[2]] + last) % 2,
                    }
                    pieces.append(piece(part, values))
        return pieces

    def finish(h):
        for g in range(8):
            rows = pl.ds(g * 256, 256)
            cols = pl.ds(pl.multiple_of((h * 8 + g) * HD, HD), HD)
            stage[:, cols] = (acc[h, rows, :] / den[h, rows, :]).astype(jnp.bfloat16)

    def halves(source, last, hooks):
        def one(h, carry):
            do(hooks, h)
            attend(pieces_of(source, (0, 1), (0, 1), last), source, h, 1024)
            return carry

        lax.fori_loop(0, 4, one, 0)

    def quarters(source, last, hooks, final=False):
        def one(it, carry):
            do(hooks, it)
            h = it % 4
            attend(pieces_of(source, (0, 1), ((it // 4,),), last), source, h, 512)
            if final:
                @pl.when(it >= 4)
                def _():
                    finish(h)
            return carry

        lax.fori_loop(0, 8, one, 0)

    quarters(ROOT, 0, {
        0: lambda: relay(steps[ROOT, 0], steps[ROOT, 1]),
        1: lambda: relay(leaf1, leaf2),
        2: lambda: relay(steps[OWN, 0], steps[OWN, 1]),
        4: lambda: relay(steps[ROOT, 1], quarter),
        6: lambda: (arrive(leaf2), choose_for_f()),
        7: lambda: start(leaf3),
    })
    halves(OWN, 0, {
        0: lambda: (relay(steps[OWN, 1], steps[OWN, 2]), start(steps[OWN, 3])),
        1: lambda: (arrive(quarter), start(round1)),
        3: lambda: (arrive(round1), start(round2)),
    })
    quarters(OWN, 1, {
        0: lambda: arrive(steps[OWN, 2]),
        1: lambda: (arrive(leaf3), choose_parent()),
        2: lambda: start(steps[PAR, 0]),
        4: lambda: arrive(steps[OWN, 3]),
        6: lambda: relay(steps[PAR, 0], steps[PAR, 1]),
    })
    halves(ROOT, 1, {
        0: lambda: arrive(round2),
        2: lambda: (relay(steps[PAR, 1], steps[PAR, 2]), start(steps[PAR, 3])),
    })
    halves(PAR, 0, {})
    quarters(PAR, 1, {
        0: lambda: arrive(steps[PAR, 2]),
        4: lambda: arrive(steps[PAR, 3]),
        5: lambda: send_head(0),
        6: lambda: send_head(1),
        7: lambda: send_head(2),
    }, final=True)
    send_head(3)

    for copies in (
        root_sends, own_sends, [q_send], leaf1, leaf2, leaf3, quarter, round1, round2, *steps.values()
    ):
        for copy in copies:
            copy.wait_send()
    wait_all(out_sends)
    wait_all(out_locals)


def on_device(queries, seg_keys, seg_values, root_keys, root_values, expansion, root_offsets):
    smem = pl.BlockSpec(memory_space=pltpu.SMEM)
    anywhere = pl.BlockSpec(memory_space=pl.ANY)
    return pl.pallas_call(
        kernel,
        out_shape=jax.ShapeDtypeStruct(queries.shape, jnp.bfloat16),
        in_specs=[smem, smem] + [anywhere] * 5,
        out_specs=anywhere,
        scratch_shapes=[
            pltpu.VMEM((3, 2, 2, 2, 2, 256, 512), jnp.bfloat16),
            pltpu.VMEM((256, 4096), jnp.bfloat16),
            pltpu.VMEM((2, 2, 2, 256, 512), jnp.bfloat16),
            pltpu.VMEM((2, 256, 512), jnp.bfloat16),
            pltpu.VMEM((2, 256, 512), jnp.bfloat16),
            pltpu.VMEM((4, 2048, HD), jnp.float32),
            pltpu.VMEM((4, 2048, HD), jnp.float32),
            pltpu.VMEM((4, 2048, HD), jnp.float32),
            pltpu.VMEM((256, KB), jnp.float32),
            pltpu.VMEM((256, 4096), jnp.bfloat16),
            pltpu.SemaphoreType.DMA((N_COPIES,)),
            pltpu.SemaphoreType.DMA((N_COPIES,)),
            pltpu.SemaphoreType.DMA((N_LOCAL,)),
        ],
        compiler_params=pltpu.CompilerParams(
            collective_id=0, has_side_effects=True, vmem_limit_bytes=60 * 1024 * 1024
        ),
    )(expansion, root_offsets, queries, seg_keys, seg_values, root_keys, root_values)


def solution(mesh):
    return jax.shard_map(
        on_device,
        mesh=mesh,
        in_specs=(
            P(("leaf", "ctx"), None),
            P(("leaf", "ctx"), None),
            P(("leaf", "ctx"), None),
            P("ctx", None),
            P("ctx", None),
            P(),
            P(),
        ),
        out_specs=P(("leaf", "ctx"), None),
        check_vma=False,
    )
```

time: 134 us -> 114 us (0.85)
  Pallas kernels: 131 us -> 111 us
    pallas_call x1, Pallas kernels: 131 us -> 111 us  [on_device(): pl.pallas_call(kernel, out_shape=jax.ShapeDtypeStruct(queries.shape, jnp....]
where the time goes in v2:
time: 114 us
  Pallas kernels  111 us (97%)
  local copies, waits for them, and re-layouts  3.1 us (3%)
    pallas_call x1, Pallas kernels, on_device(): pl.pallas_call(kernel, out_shape=jax.ShapeDtypeStruct(queries.shape, jnp....  111 us
    unnamed x1, local copies, waits for them, and re-layouts  3.1 us

profile of v2, /device:TPU:1, one launch (start us, length us, event | category | flops | bytes accessed | tf_op | source)
XLA Modules:
  0.0 113.8 jit_solution(9904197024486288851)
XLA Ops:
  0.0 110.7 %shard_map.73 = bf16[128,8192]{1,0:T(8,128)(2,1)} custom-call(s32[2,8]{1,0:T(2,128)} %expansion.1, s32[8]{0:T(128)} %offsets.1, bf16[128,8192]{1,0:T(8,128)(2,1)} %q_hbm.1, bf16[128,1024]{1,0:T(8,128)(2,1)} %k_hbm.1, bf16[128,1024]{1,0:T(8,128)(2,1)} %v_hbm.1, bf16[128,1024]{1,0:T(8,128)(2,1)} %rk_hbm.1, bf16[128,1024]{1,0:T(8,128)(2,1)} %rv_hbm.1), custom_call_target="tpu_custom_call" | custom-call | tf_op jit(solution)/shard_map/pallas_call | solution.py:364
  110.7 3.1 %copy.9 = bf16[128,8192]{1,0:T(8,128)(2,1)} copy(bf16[128,8192]{1,0:T(8,128)(2,1)} %shard_map.73) | data formatting | bytes 4194304

commit v3 on v2

--- a/solution.py
+++ b/solution.py
@@ -26,8 +26,6 @@
 
 N_COPIES = 61
 N_LOCAL = 14
-KB = 1024
-RB = 512
 
 
 def kernel(expansion, offsets, q_hbm, k_hbm, v_hbm, rk_hbm, rv_hbm, o_hbm,
@@ -215,6 +213,8 @@
         return first, count, pa, pb, pc, plane * 512 + pc * 256 + first
 
     def attend(pieces, source, h, kb):
+        rb = kb
+        heads = rb // 256
         columns = pl.ds(pl.multiple_of(h * HD, HD), HD)
 
         @pl.when(h == 0)
@@ -243,19 +243,19 @@
 
         def score(sb):
             rows = [
-                qbuf[:, pl.ds(pl.multiple_of((h * 8 + 2 * sb + i) * HD, HD), HD)] for i in range(2)
+                qbuf[:, pl.ds(pl.multiple_of((h * 8 + heads * sb + i) * HD, HD), HD)] for i in range(heads)
             ]
             return lax.dot_general(
                 jnp.concatenate(rows, 0), keys, (((1,), (1,)), ((), ())), preferred_element_type=jnp.float32
             )
 
         def soften(sb, s):
-            rows = pl.ds(sb * RB, RB)
+            rows = pl.ds(sb * rb, rb)
             old = top[h, rows, :]
             limited, best = [], None
             for j in range(kb // 128):
                 lim = bound[:, j * 128:(j + 1) * 128]
-                sj = jnp.minimum(s[:, j * 128:(j + 1) * 128], jnp.concatenate([lim, lim], 0))
+                sj = jnp.minimum(s[:, j * 128:(j + 1) * 128], jnp.concatenate([lim] * heads, 0))
                 limited.append(sj)
                 best = sj if best is None else jnp.maximum(best, sj)
             new = jnp.maximum(old, jnp.max(best, axis=1, keepdims=True))
@@ -268,8 +268,8 @@
             top[h, rows, :] = new
 
         s = score(0)
-        for sb in range(4):
-            following = score(sb + 1) if sb < 3 else None
+        for sb in range(2048 // rb):
+            following = score(sb + 1) if sb + 1 < 2048 // rb else None
             soften(sb, s)
             s = following
 
@@ -294,23 +294,21 @@
             cols = pl.ds(pl.multiple_of((h * 8 + g) * HD, HD), HD)
             stage[:, cols] = (acc[h, rows, :] / den[h, rows, :]).astype(jnp.bfloat16)
 
-    def halves(source, last, hooks):
+    def halves(source, last, hooks, final=False):
         def one(h, carry):
             do(hooks, h)
             attend(pieces_of(source, (0, 1), (0, 1), last), source, h, 1024)
+            if final:
+                finish(h)
             return carry
 
         lax.fori_loop(0, 4, one, 0)
 
-    def quarters(source, last, hooks, final=False):
+    def quarters(source, last, hooks):
         def one(it, carry):
             do(hooks, it)
             h = it % 4
             attend(pieces_of(source, (0, 1), ((it // 4,),), last), source, h, 512)
-            if final:
-                @pl.when(it >= 4)
-                def _():
-                    finish(h)
             return carry
 
         lax.fori_loop(0, 8, one, 0)
@@ -340,12 +338,11 @@
         2: lambda: (relay(steps[PAR, 1], steps[PAR, 2]), start(steps[PAR, 3])),
     })
     halves(PAR, 0, {})
-    quarters(PAR, 1, {
-        0: lambda: arrive(steps[PAR, 2]),
-        4: lambda: arrive(steps[PAR, 3]),
-        5: lambda: send_head(0),
-        6: lambda: send_head(1),
-        7: lambda: send_head(2),
+    halves(PAR, 1, {
+        0: lambda: (arrive(steps[PAR, 2]), arrive(steps[PAR, 3])),
+        1: lambda: send_head(0),
+        2: lambda: send_head(1),
+        3: lambda: send_head(2),
     }, final=True)
     send_head(3)
 
@@ -375,7 +372,7 @@
             pltpu.VMEM((4, 2048, HD), jnp.float32),
             pltpu.VMEM((4, 2048, HD), jnp.float32),
             pltpu.VMEM((4, 2048, HD), jnp.float32),
-            pltpu.VMEM((256, KB), jnp.float32),
+            pltpu.VMEM((256, 1024), jnp.float32),
             pltpu.VMEM((256, 4096), jnp.bfloat16),
             pltpu.SemaphoreType.DMA((N_COPIES,)),
             pltpu.SemaphoreType.DMA((N_COPIES,)),

time: 114 us -> 110 us (0.965)
  Pallas kernels: 111 us -> 106 us
    pallas_call x1, Pallas kernels: 111 us -> 106 us  [on_device(): pl.pallas_call(kernel, out_shape=jax.ShapeDtypeStruct(queries.shape, jnp....]
where the time goes in v3:
time: 110 us; the launch traced here: 109 us
  Pallas kernels  106 us (96%)
  local copies, waits for them, and re-layouts  3.1 us (3%)
    pallas_call x1, Pallas kernels, on_device(): pl.pallas_call(kernel, out_shape=jax.ShapeDtypeStruct(queries.shape, jnp....  106 us
    unnamed x1, local copies, waits for them, and re-layouts  3.1 us

profile of v3, /device:TPU:1, one launch (start us, length us, event | category | flops | bytes accessed | tf_op | source)
XLA Modules:
  0.0 109.4 jit_solution(16687021240236283167)
XLA Ops:
  0.0 106.3 %shard_map.73 = bf16[128,8192]{1,0:T(8,128)(2,1)} custom-call(s32[2,8]{1,0:T(2,128)} %expansion.1, s32[8]{0:T(128)} %offsets.1, bf16[128,8192]{1,0:T(8,128)(2,1)} %q_hbm.1, bf16[128,1024]{1,0:T(8,128)(2,1)} %k_hbm.1, bf16[128,1024]{1,0:T(8,128)(2,1)} %v_hbm.1, bf16[128,1024]{1,0:T(8,128)(2,1)} %rk_hbm.1, bf16[128,1024]{1,0:T(8,128)(2,1)} %rv_hbm.1), custom_call_target="tpu_custom_call" | custom-call | tf_op jit(solution)/shard_map/pallas_call | solution.py:361
  106.3 3.1 %copy.9 = bf16[128,8192]{1,0:T(8,128)(2,1)} copy(bf16[128,8192]{1,0:T(8,128)(2,1)} %shard_map.73) | data formatting | bytes 4194304

commit v4 on v3

--- a/solution.py
+++ b/solution.py
@@ -89,13 +89,16 @@
 
     both = slice(None)
 
+    def toward(source, dim):
+        return near_f if source == ROOT and dim == 2 else near[dim]
+
     def double(source, part, step, second=None):
         order = order_of(source, part)
         where = {dim: both if dim in order[:step] else bits[dim] for dim in range(3)}
         if second is not None:
             where[order[1]] = second
         slot = block(source, part, where)
-        return remote(slot, slot, near[order[step]])
+        return remote(slot, slot, toward(source, order[step]))
 
     steps = {}
     for source in (ROOT, OWN, PAR):
@@ -114,7 +117,7 @@
     for part in range(3):
         last = order_of(ROOT, part)[2]
         slot = shared(part, d, e, bits[last])
-        quarter.append(remote(slot, slot, near[last]))
+        quarter.append(remote(slot, slot, toward(ROOT, last)))
         flip = 1 - bits[last]
         for t, (one_way, other_way) in enumerate(((near_d, near_e), (near_e, near_d))):
             slot = shared(part, d, e, flip, t)

time: 110 us -> 108 us (0.982)
    pallas_call x1, Pallas kernels: 106 us -> 105 us  [on_device(): pl.pallas_call(kernel, out_shape=jax.ShapeDtypeStruct(queries.shape, jnp....]
where the time goes in v4:
time: 108 us
  Pallas kernels  105 us (97%)
  local copies, waits for them, and re-layouts  3.1 us (3%)
    pallas_call x1, Pallas kernels, on_device(): pl.pallas_call(kernel, out_shape=jax.ShapeDtypeStruct(queries.shape, jnp....  105 us
    unnamed x1, local copies, waits for them, and re-layouts  3.1 us

profile of v4, /device:TPU:1, one launch (start us, length us, event | category | flops | bytes accessed | tf_op | source)
XLA Modules:
  0.0 108.0 jit_solution(11000864587399914573)
XLA Ops:
  0.0 104.9 %shard_map.73 = bf16[128,8192]{1,0:T(8,128)(2,1)} custom-call(s32[2,8]{1,0:T(2,128)} %expansion.1, s32[8]{0:T(128)} %offsets.1, bf16[128,8192]{1,0:T(8,128)(2,1)} %q_hbm.1, bf16[128,1024]{1,0:T(8,128)(2,1)} %k_hbm.1, bf16[128,1024]{1,0:T(8,128)(2,1)} %v_hbm.1, bf16[128,1024]{1,0:T(8,128)(2,1)} %rk_hbm.1, bf16[128,1024]{1,0:T(8,128)(2,1)} %rv_hbm.1), custom_call_target="tpu_custom_call" | custom-call | tf_op jit(solution)/shard_map/pallas_call | solution.py:364
  104.9 3.1 %copy.9 = bf16[128,8192]{1,0:T(8,128)(2,1)} copy(bf16[128,8192]{1,0:T(8,128)(2,1)} %shard_map.73) | data formatting | bytes 4194304
